TPU v7x, 32 devices: a whole 2x2x4 slice. The times are simulated.
32 devices in a mesh: dp: 8 (over z, y), expert: 4 (over x, core).
Axes of the slice: x: 2, y: 2, z: 4, core: 2. Of those that a mesh axis runs over, the one named last changes fastest.
Arguments:
- tokens: bfloat16 [4096, 2048], P(('dp', 'expert')), may hold values from -6 to 6
- expert_ids: int32 [4096, 1], P(('dp', 'expert')), may hold values from 0 to 1
- copy_choice: int32 [4096, 1], P(('dp', 'expert')), may hold values from 0 to 1
- gate_weights: float32 [4096, 1], P(('dp', 'expert')), may hold values from 0.05 to 1
- w_gate: bfloat16 [2048, 3072], P(None, 'expert'), may hold values from -0.125 to 0.125
- w_up: bfloat16 [2048, 3072], P(None, 'expert'), may hold values from -0.125 to 0.125
- w_down: bfloat16 [3072, 2048], P('expert'), may hold values from -0.15625 to 0.15625
Outputs:
- moe_out: bfloat16 [4096, 2048], P(('dp', 'expert'))
- expert_load: float32 [2], replicated
Inputs may be any that keep to these rules, and one draw needn't show every extreme that they name: `expert_ids`: the 1 expert of a token are distinct.
All inputs are finite; a program needn't handle non-finite values.
Results may differ from a plain program's by a relative error of at most 0.0049.
Values may be sent and summed in bfloat16 or wider, within the bound.
No kernel may reach another device: no remote copies, remote signals or barrier semaphores. Data moves between devices by JAX's collectives and lax.ppermute only.
A program may use at most 64 MiB of HBM per device.

v0:
```python
import jax
import jax.numpy as jnp
from jax import lax
from jax.sharding import PartitionSpec as P


def partner(value, axis, distance):
    mask = 2**distance
    pairs = [(source, source ^ mask) for source in range(lax.axis_size(axis))]
    return lax.ppermute(value, axis, pairs)


def expert_pass(inputs, weight_gate, weight_up, weight_down):
    gate_act = jnp.dot(inputs, weight_gate, preferred_element_type=jnp.float32)
    up_act = jnp.dot(inputs, weight_up, preferred_element_type=jnp.float32)
    hidden = (jax.nn.silu(gate_act) * up_act).astype(jnp.bfloat16)
    return jnp.dot(hidden, weight_down, preferred_element_type=jnp.float32)


def local(tokens, expert_ids, copy_choice, gate_weights, w_gate, w_up, w_down):
    members = lax.axis_size("expert")
    experts = members // 2
    tok_rows, chosen = expert_ids.shape
    features = tokens.shape[1]
    capacity = max(2, tok_rows * chosen // (2 * experts))
    sections = 2 * experts
    route_keys = (expert_ids * 2 + copy_choice).reshape(-1)
    onehot = (route_keys[:, None] == jnp.arange(sections, dtype=jnp.int32)[None, :]).astype(
        jnp.int32
    )
    before = jnp.cumsum(onehot, axis=0) - onehot
    slot_rank = jnp.sum(before * onehot, axis=1)
    retained = slot_rank < capacity
    target = jnp.where(retained, route_keys * capacity + slot_rank, -1).reshape(tok_rows, chosen)
    places = jnp.arange(sections * capacity, dtype=jnp.int32)
    matches = places[:, None, None] == target[None, :, :]
    dispatch = jnp.sum(matches.astype(jnp.float32), axis=2).astype(jnp.bfloat16)
    packed = jnp.dot(dispatch, tokens, preferred_element_type=jnp.float32).astype(jnp.bfloat16)
    packed = packed.reshape(experts, 2, capacity, features)
    primary = packed[:, 0]
    spare_rows = packed[:, 1]
    spare_gate, spare_up, spare_down = (w_gate, w_up, w_down)
    outgoing = jnp.repeat(jnp.stack([primary, spare_rows], axis=1), 2, axis=0)
    arrived = lax.all_to_all(outgoing, "expert", split_axis=0, concat_axis=0, tiled=True)
    sources = arrived.shape[0]
    slot_count = arrived.shape[2]
    first_part = expert_pass(arrived[:, 0].reshape(-1, features), w_gate, w_up, w_down)
    second = expert_pass(arrived[:, 1].reshape(-1, features), spare_gate, spare_up, spare_down)
    partials = jnp.stack(
        [
            first_part.reshape(sources, slot_count, features),
            second.reshape(sources, slot_count, features),
        ],
        axis=1,
    )
    core_half = lax.axis_index("expert") % 2
    own_part = lax.dynamic_index_in_dim(partials, core_half, 1, keepdims=False)
    partner_part = lax.dynamic_index_in_dim(partials, 1 - core_half, 1, keepdims=False)
    merged = own_part + partner(partner_part, "expert", 0)
    returned = lax.all_to_all(merged, "expert", split_axis=0, concat_axis=0, tiled=True)
    results = returned.reshape(experts, 2, slot_count, features)
    first_back = results[:, 0]
    second_back = results[:, 1]
    outputs = jnp.stack([first_back, second_back], axis=1).reshape(sections * capacity, features)
    scaled = jnp.sum(jnp.where(matches, gate_weights[None, :, :], 0.0), axis=2)
    combined = jnp.einsum(
        "st,sd->td",
        scaled,
        outputs,
        precision=lax.Precision.HIGHEST,
        preferred_element_type=jnp.float32,
    )
    kept_gate = jnp.where(retained.reshape(tok_rows, chosen), gate_weights, 0.0)
    expert_match = expert_ids[:, :, None] == jnp.arange(experts, dtype=jnp.int32)[None, None, :]
    local_load = jnp.sum(jnp.where(expert_match, kept_gate[:, :, None], 0.0), axis=(0, 1))
    load_sum = lax.psum(local_load, ("dp", "expert"))
    expert_load = load_sum / (tok_rows * lax.axis_size("dp") * members)
    return (combined.astype(jnp.bfloat16), expert_load)


def solution(mesh):
    return jax.shard_map(
        local,
        mesh=mesh,
        in_specs=(
            P(("dp", "expert"), None),
            P(("dp", "expert"), None),
            P(("dp", "expert"), None),
            P(("dp", "expert"), None),
            P(None, "expert"),
            P(None, "expert"),
            P("expert", None),
        ),
        out_specs=(P(("dp", "expert"), None), P()),
        check_vma=False,
    )
```

profile of v0, /device:TPU:0, one launch (start us, length us, event | category | flops | bytes accessed | tf_op | source)
XLA Modules:
  0.0 104.1 jit_solution(1583701060914143018)
XLA Ops:
  0.6 0.0 copy-start
  0.6 0.8 add_bitcast_fusion
  1.5 0.1 fusion.23
  1.6 0.2 reduce_window_sum.11
  1.7 0.2 select_reduce_fusion
  1.9 1.3 %convolution_convert_fusion.1 = bf16[128,2048]{1,0:T(8,128)(2,1)S(1)} fusion(bf16[128,2048]{1,0:T(8,128)(2,1)} %param.7, s32[128]{0:T(128)S(1)} %compare_select_fusion.1), kind=kOutput, calls=%fused_computation.5 | convolution fusion | flops 67420160 | bytes 1049088 | tf_op jit(solution)/shard_map/dot_general | solution.py:38
  3.3 1.2 %broadcast_in_dim.44 = bf16[2,2,2,32,2048]{4,3,2,1,0:T(8,128)(2,1)} broadcast(bf16[2,2,32,2048]{3,2,1,0:T(8,128)(2,1)S(1)} %bitcast.47), dimensions={0,2,3,4} | broadcast | bytes 1572864 | tf_op jit(solution)/shard_map/broadcast_in_dim | solution.py:43
  4.4 4.2 %all-to-all-start = ((bf16[4,2,32,2048]{3,2,1,0:T(8,128)(2,1)}), bf16[4,2,32,2048]{3,2,1,0:T(8,128)(2,1)}, u32[]{:S(2)}, u32[]{:S(2)}) async-start(bf16[4,2,32,2048]{3,2,1,0:T(8,128)(2,1)} %bitcast.46), calls=%async_computation | async-start | bytes 2097152 | tf_op jit(solution)/shard_map/all_to_all | solution.py:44
  8.7 15.2 %all-to-all-done = bf16[4,2,32,2048]{3,2,1,0:T(8,128)(2,1)} async-done(((bf16[4,2,32,2048]{3,2,1,0:T(8,128)(2,1)}), bf16[4,2,32,2048]{3,2,1,0:T(8,128)(2,1)}, u32[]{:S(2)}, u32[]{:S(2)}) %all-to-all-start) | async-done | bytes 1048608 | tf_op jit(solution)/shard_map/all_to_all | solution.py:44
  23.8 0.0 copy-start.1
  23.8 1.4 %fusion.33 = (bf16[4,1,32,2048]{3,2,1,0:T(8,128)(2,1)S(1)}, bf16[4,1,32,2048]{3,2,1,0:T(8,128)(2,1)S(1)}) fusion(bf16[4,2,32,2048]{3,2,1,0:T(8,128)(2,1)} %all-to-all-done), kind=kLoop, calls=%fused_computation.51 | loop fusion | bytes 2097152 | tf_op jit(solution)/shard_map/slice | solution.py:48
  25.3 0.0 copy-start.3
  25.3 0.0 copy-start.2
  25.3 0.8 copy-done.3
  26.1 3.2 %fusion.34 = f32[128,768]{1,0:T(8,128)} fusion(bf16[128,2048]{1,0:T(8,128)(2,1)S(1)} %bitcast.44, bf16[2048,768]{1,0:T(8,128)(2,1)} %param.11), kind=kOutput, calls=%fused_computation.52 | convolution fusion | flops 402653184 | bytes 4063232 | tf_op jit(solution)/shard_map/dot_general | solution.py:14
  29.3 0.0 copy-done.2
  29.3 0.0 copy-done.1
  29.3 0.6 fusion.35
  29.9 0.0 copy-done
  29.9 4.3 %fusion.3 = f32[128,2048]{1,0:T(8,128)} fusion(bf16[768,2048]{1,0:T(8,128)(2,1)S(1)} %copy-done, bf16[128,2048]{1,0:T(8,128)(2,1)} %bitcast.45, bf16[2048,768]{1,0:T(8,128)(2,1)} %param.12, f32[128,768]{1,0:T(8,128)} %fusion.34), kind=kOutput, calls=%fused_computation.11 | convolution fusion | flops 805896192 | bytes 8257536 | tf_op jit(solution)/shard_map/dot_general | solution.py:17
  34.2 4.3 %fusion.2 = f32[128,2048]{1,0:T(8,128)} fusion(bf16[768,2048]{1,0:T(8,128)(2,1)S(1)} %copy-done, bf16[128,2048]{1,0:T(8,128)(2,1)} %bitcast.43, bf16[2048,768]{1,0:T(8,128)(2,1)} %param.12, f32[128,768]{1,0:T(8,128)S(1)} %fusion.35), kind=kOutput, calls=%fused_computation.10 | convolution fusion | flops 805896192 | bytes 8257536 | tf_op jit(solution)/shard_map/dot_general | solution.py:17
  38.6 2.4 %fusion.5 = f32[4,32,2048]{2,1,0:T(8,128)} fusion(s32[]{:T(128)S(6)} %select_n.67, f32[4,1,32,2048]{3,2,0,1:T(8,128)} %bitcast.38, f32[4,1,32,2048]{3,2,0,1:T(8,128)} %bitcast.40), kind=kLoop, calls=%fused_computation.13 | loop fusion | flops 262144 | bytes 3145732 | tf_op jit(solution)/shard_map/jit(dynamic_index_in_dim)/squeeze | solution.py:58
  41.0 0.0 collective-permute-start
  41.0 0.0 copy-start.4
  41.0 0.0 copy-start.5
  41.0 3.0 %collective-permute-done = f32[4,32,2048]{2,1,0:T(8,128)} collective-permute-done((f32[4,32,2048]{2,1,0:T(8,128)}, f32[4,32,2048]{2,1,0:T(8,128)}, u32[]{:S(2)}, u32[]{:S(2)}) %collective-permute-start) | collective-permute-done | bytes 1048608 | tf_op jit(solution)/shard_map/ppermute | solution.py:10
  44.0 2.8 %fusion.8 = f32[4,32,2048]{2,1,0:T(8,128)} fusion(f32[4,32,2048]{2,1,0:T(8,128)} %collective-permute-done, s32[]{:T(128)S(6)} %select_n.66, f32[4,1,32,2048]{3,2,0,1:T(8,128)} %bitcast.39, f32[4,1,32,2048]{3,2,0,1:T(8,128)} %bitcast.41), kind=kLoop, calls=%fused_computation.16 | loop fusion | flops 524288 | bytes 4194308 | tf_op jit(solution)/shard_map/add | solution.py:59
  46.7 4.2 %all-to-all-start.1 = ((f32[4,32,2048]{2,1,0:T(8,128)}), f32[4,32,2048]{2,1,0:T(8,128)}, u32[]{:S(2)}, u32[]{:S(2)}) async-start(f32[4,32,2048]{2,1,0:T(8,128)} %fusion.8), calls=%async_computation.1 | async-start | bytes 2097152 | tf_op jit(solution)/shard_map/all_to_all | solution.py:60
  51.0 0.0 copy-done.4
  51.0 0.0 copy-done.5
  51.0 0.1 fusion.28
  51.1 49.4 %psum.7 = f32[2]{0:T(128)S(1)} all-reduce(f32[2]{0:T(128)S(1)} %fusion.28), channel_id=1, replica_groups=mesh['dp'=8,'expert'=4] {'dp','expert'}, use_global_device_ids=true, to_apply=%region_3.4 | all-reduce | flops 2 | bytes 16 | tf_op jit(solution)/shard_map/psum | solution.py:76
  100.6 0.5 broadcast_multiply_fusion
  101.1 0.0 all-to-all-done.1
  101.1 3.1 %convolution_convert_fusion = bf16[128,2048]{1,0:T(8,128)(2,1)} fusion(f32[128,2048]{1,0:T(8,128)} %bitcast.11, f32[128]{0:T(128)S(1)} %bitcast.48, s32[128]{0:T(128)S(1)} %compare_select_fusion.1), kind=kOutput, calls=%fused_computation.4 | convolution fusion | flops 402948096 | bytes 1573888 | tf_op jit(solution)/shard_map/st,sd->td/dot_general | solution.py:66
  (2 shorter events, 0.0 us)
Async XLA Ops:
  0.6 29.3 %copy-start = (bf16[768,2048]{1,0:T(8,128)(2,1)S(1)}, bf16[768,2048]{1,0:T(8,128)(2,1)}, u32[]{:S(2)}) copy-start(bf16[768,2048]{1,0:T(8,128)(2,1)} %param.13) | copy-start | bytes 9437188
  4.4 19.4 %all-to-all-start = ((bf16[4,2,32,2048]{3,2,1,0:T(8,128)(2,1)}), bf16[4,2,32,2048]{3,2,1,0:T(8,128)(2,1)}, u32[]{:S(2)}, u32[]{:S(2)}) async-start(bf16[4,2,32,2048]{3,2,1,0:T(8,128)(2,1)} %bitcast.46), calls=%async_computation | async-start | bytes 2097152 | tf_op jit(solution)/shard_map/all_to_all | solution.py:44
  23.8 5.5 %copy-start.1 = (bf16[2048,768]{1,0:T(8,128)(2,1)S(1)}, bf16[2048,768]{1,0:T(8,128)(2,1)}, u32[]{:S(2)}) copy-start(bf16[2048,768]{1,0:T(8,128)(2,1)} %param.11) | copy-start | bytes 9437188
  25.3 0.8 copy-start.3
  25.3 4.0 %copy-start.2 = (bf16[4,1,32,2048]{3,2,1,0:T(8,128)(2,1)}, bf16[4,1,32,2048]{3,2,1,0:T(8,128)(2,1)S(1)}, u32[]{:S(2)}) copy-start(bf16[4,1,32,2048]{3,2,1,0:T(8,128)(2,1)S(1)} %get-tuple-element.2) | copy-start | bytes 1572868
  41.0 3.0 %collective-permute-start = (f32[4,32,2048]{2,1,0:T(8,128)}, f32[4,32,2048]{2,1,0:T(8,128)}, u32[]{:S(2)}, u32[]{:S(2)}) collective-permute-start(f32[4,32,2048]{2,1,0:T(8,128)} %fusion.5), channel_id=1, source_target_pairs={{0,1},{1,0},{2,3},{3,2},{4,5},{5,4},{6,7},{7,6},{8,9},{9,8},{10,11... | collective-permute-start | bytes 3145736 | tf_op jit(solution)/shard_map/ppermute | solution.py:10
  41.0 10.0 %copy-start.4 = (f32[128,1]{0,1:T(1,128)S(1)}, f32[128,1]{0,1:T(1,128)}, u32[]{:S(2)}) copy-start(f32[128,1]{0,1:T(1,128)} %param.10) | copy-start | bytes 1540
  41.0 10.0 %copy-start.5 = (s32[128,1]{0,1:T(1,128)S(1)}, s32[128,1]{0,1:T(1,128)}, u32[]{:S(2)}) copy-start(s32[128,1]{0,1:T(1,128)} %param.8) | copy-start | bytes 1540
  46.7 54.4 %all-to-all-start.1 = ((f32[4,32,2048]{2,1,0:T(8,128)}), f32[4,32,2048]{2,1,0:T(8,128)}, u32[]{:S(2)}, u32[]{:S(2)}) async-start(f32[4,32,2048]{2,1,0:T(8,128)} %fusion.8), calls=%async_computation.1 | async-start | bytes 2097152 | tf_op jit(solution)/shard_map/all_to_all | solution.py:60
where the time goes:
time: 105 us; the launch traced here: 104 us
  blocking collectives  49.4 us (47%)
  waiting for transfers between devices  18.1 us (17%)
  matrix products  16.9 us (16%)
  starting transfers between devices  8.47 us (8%)
  other arithmetic  7.01 us (7%)
  local copies, waits for them, and re-layouts  3.38 us (3%)
    psum x1, blocking collectives, local(): load_sum = lax.psum(local_load, ('dp', 'expert'))  49.4 us
    all_to_all x1, waiting for transfers between devices, local(): lax.all_to_all(outgoing, 'expert', split_axis=0, concat_axis=0, tiled=True)  15.2 us
    dot_general x2, matrix products, expert_pass(): return jnp.dot(hidden, weight_down, preferred_element_type=jnp.float32)  8.7 us
    all_to_all x1, starting transfers between devices, local(): lax.all_to_all(outgoing, 'expert', split_axis=0, concat_axis=0, tiled=True)  4.24 us
    all_to_all x1, starting transfers between devices, local(): lax.all_to_all(merged, 'expert', split_axis=0, concat_axis=0, tiled=True)  4.24 us
    dot_general x2, matrix products, expert_pass(): gate_act = jnp.dot(inputs, weight_gate, preferred_element_type=jnp.float32)  3.81 us
    dot_general x1, matrix products, local(): jnp.einsum('st,sd->td', scaled, outputs, precision=lax.Precision.HIGHEST,...  3.05 us
    ppermute x1, waiting for transfers between devices, partner(): return lax.ppermute(value, axis, pairs)  2.99 us
  transfers between devices with their start and end apart: 3, of which 2 were waited for; matrix products, arithmetic and copies ran while one was open for 1% of the time, Pallas kernels for 0%

commit v1 on v0

v1 whole, which is shorter than its diff:
```python
import jax
import jax.numpy as jnp
from jax import lax
from jax.sharding import PartitionSpec as P


def swap(value, axis, mask):
    pairs = [(source, source ^ mask) for source in range(lax.axis_size(axis))]
    return lax.ppermute(value, axis, pairs)


def shift(value, step):
    members = lax.axis_size("expert")
    pairs = [(source, (source + 2 * step) % members) for source in range(members)]
    return lax.ppermute(value, "expert", pairs)


def tree_sum(value, axis):
    terms = [value] + [swap(value, axis, mask) for mask in range(1, lax.axis_size(axis))]
    while len(terms) > 1:
        terms = [terms[i] + terms[i + 1] for i in range(0, len(terms), 2)]
    return terms[0]


def expert_pass(inputs, weight_gate, weight_up, weight_down):
    gate_act = jnp.dot(inputs, weight_gate, preferred_element_type=jnp.float32)
    up_act = jnp.dot(inputs, weight_up, preferred_element_type=jnp.float32)
    hidden = (jax.nn.silu(gate_act) * up_act).astype(jnp.bfloat16)
    return jnp.dot(hidden, weight_down, preferred_element_type=jnp.float32)


def local(tokens, expert_ids, copy_choice, gate_weights, w_gate, w_up, w_down):
    members = lax.axis_size("expert")
    experts = members // 2
    tok_rows, chosen = expert_ids.shape
    features = tokens.shape[1]
    capacity = max(2, tok_rows * chosen // (2 * experts))
    rows = 2 * capacity
    sections = 2 * experts
    own_expert = lax.axis_index("expert") // 2
    relative = expert_ids - own_expert
    relative = jnp.where(relative < 0, relative + experts, relative)
    route_keys = (relative * 2 + copy_choice).reshape(-1)
    onehot = (route_keys[:, None] == jnp.arange(sections, dtype=jnp.int32)[None, :]).astype(
        jnp.int32
    )
    before = jnp.cumsum(onehot, axis=0) - onehot
    slot_rank = jnp.sum(before * onehot, axis=1)
    retained = slot_rank < capacity
    target = jnp.where(retained, route_keys * capacity + slot_rank, -1).reshape(tok_rows, chosen)
    places = jnp.arange(sections * capacity, dtype=jnp.int32)
    matches = places[:, None, None] == target[None, :, :]
    dispatch = jnp.any(matches, axis=2).astype(jnp.bfloat16)
    packed = jnp.dot(dispatch, tokens, preferred_element_type=jnp.float32).astype(jnp.bfloat16)
    packed = packed.reshape(experts, rows, features)

    arrived = [shift(packed[step], step) for step in range(1, experts)]
    kept_gate = jnp.where(retained.reshape(tok_rows, chosen), gate_weights, 0.0)
    expert_match = expert_ids[:, :, None] == jnp.arange(experts, dtype=jnp.int32)[None, None, :]
    local_load = jnp.sum(jnp.where(expert_match, kept_gate[:, :, None], 0.0), axis=(0, 1))
    load_sum = tree_sum(tree_sum(local_load, "expert"), "dp")
    expert_load = load_sum / (tok_rows * lax.axis_size("dp") * members)

    def serve(mine):
        count = mine.shape[0]
        both = jnp.concatenate([mine, swap(mine, "expert", 1)], axis=0)
        partial = expert_pass(both, w_gate, w_up, w_down)
        other = swap(partial[count:].astype(jnp.bfloat16), "expert", 1)
        return (partial[:count] + other.astype(jnp.float32)).astype(jnp.bfloat16)

    near = serve(packed[0])
    far = serve(jnp.concatenate(arrived, axis=0))
    returned = [shift(far[(step - 1) * rows : step * rows], -step) for step in range(1, experts)]
    outputs = jnp.concatenate([near] + returned, axis=0)
    combined = jnp.zeros((tok_rows, features), jnp.float32)
    for choice in range(chosen):
        select = (target[:, choice : choice + 1] == places[None, :]).astype(jnp.bfloat16)
        chosen_rows = jnp.dot(select, outputs, preferred_element_type=jnp.float32)
        combined = combined + gate_weights[:, choice : choice + 1] * chosen_rows
    return (combined.astype(jnp.bfloat16), expert_load)


def solution(mesh):
    return jax.shard_map(
        local,
        mesh=mesh,
        in_specs=(
            P(("dp", "expert"), None),
            P(("dp", "expert"), None),
            P(("dp", "expert"), None),
            P(("dp", "expert"), None),
            P(None, "expert"),
            P(None, "expert"),
            P("expert", None),
        ),
        out_specs=(P(("dp", "expert"), None), P()),
        check_vma=False,
    )
```

time: 105 us -> 54.8 us (0.52)
  blocking collectives: 49.4 us -> 0 us
  starting transfers between devices: 8.47 us -> 19.1 us
  waiting for transfers between devices: 18.1 us -> 10.3 us
  matrix products: 16.9 us -> 14.9 us
  other arithmetic: 7.01 us -> 5.49 us
    psum x1 -> x0, blocking collectives: 49.4 us -> none  [local(): load_sum = lax.psum(local_load, ('dp', 'expert'))]
    ppermute x1 -> x16, starting transfers between devices: 0.01 us -> 19.1 us  [the longest x14 16.6 us: swap(): return lax.ppermute(value, axis, pairs)]
    all_to_all x2 -> x0, waiting for transfers between devices: 15.2 us -> none  [the longest x1 15.2 us: local(): lax.all_to_all(outgoing, 'expert', split_axis=0, concat_axis=0, tiled=True)]
    all_to_all x2 -> x0, starting transfers between devices: 8.47 us -> none  [the longest x1 4.24 us: local(): lax.all_to_all(outgoing, 'expert', split_axis=0, concat_axis=0, tiled=True)]
    ppermute x1 -> x16, waiting for transfers between devices: 2.99 us -> 10.3 us  [the longest x2 7.05 us: shift(): return lax.ppermute(value, 'expert', pairs)]
    squeeze x1 -> x0, other arithmetic: 2.36 us -> none  [local(): lax.dynamic_index_in_dim(partials, 1 - core_half, 1, keepdims=False)]
    convert_element_type x0 -> x2, other arithmetic: none -> 2.26 us  [serve(): return (partial[:count] + other.astype(jnp.float32)).astype(jnp.bfloat16)]
    add x1 -> x2, other arithmetic: 2.76 us -> 0.84 us  [the longest x1 0.83 us: local(): route_keys = (relative * 2 + copy_choice).reshape(-1)]
  transfers between devices with their start and end apart: 3 -> 16, of which waited for: 2 -> 2; matrix products, arithmetic and copies ran while one was open for 1% -> 24% of each run, Pallas kernels for 0% -> 0%
where the time goes in v1:
time: 54.8 us; the launch traced here: 54.4 us
  starting transfers between devices  19.1 us (35%)
  matrix products  14.9 us (27%)
  waiting for transfers between devices  10.3 us (19%)
  other arithmetic  5.49 us (10%)
  local copies, waits for them, and re-layouts  3.75 us (7%)
  between operations  0.82 us (1%)
    ppermute x14, starting transfers between devices, swap(): return lax.ppermute(value, axis, pairs)  16.6 us
    dot_general x2, matrix products, expert_pass(): return jnp.dot(hidden, weight_down, preferred_element_type=jnp.float32)  8.67 us
    ppermute x2, waiting for transfers between devices, shift(): return lax.ppermute(value, 'expert', pairs)  7.05 us
    dot_general x2, matrix products, expert_pass(): gate_act = jnp.dot(inputs, weight_gate, preferred_element_type=jnp.float32)  3.8 us
    ppermute x14, waiting for transfers between devices, swap(): return lax.ppermute(value, axis, pairs)  3.25 us
    ppermute x2, starting transfers between devices, shift(): return lax.ppermute(value, 'expert', pairs)  2.56 us
    convert_element_type x2, other arithmetic, serve(): return (partial[:count] + other.astype(jnp.float32)).astype(jnp.bfloat16)  2.26 us
    slice x2, local copies, waits for them, and re-layouts, serve(): other = swap(partial[count:].astype(jnp.bfloat16), 'expert', 1)  2.14 us
  transfers between devices with their start and end apart: 16, of which 2 were waited for; matrix products, arithmetic and copies ran while one was open for 24% of the time, Pallas kernels for 0%

profile of v1, /device:TPU:0, one launch (start us, length us, event | category | flops | bytes accessed | tf_op | source)
XLA Modules:
  0.0 54.4 jit_solution(15392928543915783665)
XLA Ops:
  0.6 0.0 copy-start
  0.7 0.8 %fusion.19 = s32[128,1]{0,1:T(1,128)S(1)} fusion(s32[128,1]{0,1:T(1,128)} %param.9, s32[128,1]{0,1:T(1,128)} %param.8, s32[]{:T(128)S(6)} %select_n.38), kind=kLoop, calls=%fused_computation.39 | loop fusion | flops 768 | bytes 1540 | tf_op jit(solution)/shard_map/add | solution.py:43
  1.5 0.1 fusion.12
  1.6 0.2 reduce_window_sum.11
  1.8 0.2 select_reduce_fusion
  1.9 0.7 %fusion.17 = f32[128]{0:T(128)S(1)} fusion(f32[128,1]{0,1:T(1,128)} %param.10, s32[128]{0:T(128)S(1)} %select_reduce_fusion), kind=kLoop, calls=%fused_computation.37 | loop fusion | flops 256 | bytes 1536 | tf_op jit(solution)/shard_map/jit(_where)/select_n | solution.py:58
  2.6 0.8 %fusion.15 = f32[2]{0:T(128)S(1)} fusion(f32[128]{0:T(128)S(1)} %fusion.17, s32[128]{0:T(128)} %bitcast.25), kind=kLoop, calls=%fused_computation.35 | loop fusion | flops 766 | bytes 1032 | tf_op jit(solution)/shard_map/reduce_sum | solution.py:60
  3.4 0.6 %collective-permute-start.6 = (f32[2]{0:T(128)S(1)}, f32[2]{0:T(128)S(1)}, u32[]{:S(2)}, u32[]{:S(2)}) collective-permute-start(f32[2]{0:T(128)S(1)} %fusion.15), channel_id=1, source_target_pairs={{0,1},{1,0},{2,3},{3,2},{4,5},{5,4},{6,7},{7,6},{8,9},{9,8},{10,11... | collective-permute-start | bytes 32 | tf_op jit(solution)/shard_map/ppermute | solution.py:9
  3.9 2.6 %collective-permute-start.7 = (f32[2]{0:T(128)S(1)}, f32[2]{0:T(128)S(1)}, u32[]{:S(2)}, u32[]{:S(2)}) collective-permute-start(f32[2]{0:T(128)S(1)} %fusion.15), channel_id=1, source_target_pairs={{0,2},{1,3},{2,0},{3,1},{4,6},{5,7},{6,4},{7,5},{8,10},{9,11},{10,... | collective-permute-start | bytes 32 | tf_op jit(solution)/shard_map/ppermute | solution.py:9
  6.5 0.0 collective-permute-start.8
  6.5 1.3 %convolution_convert_fusion = bf16[128,2048]{1,0:T(8,128)(2,1)S(1)} fusion(bf16[128,2048]{1,0:T(8,128)(2,1)} %param.7, s32[128]{0:T(128)S(1)} %compare_select_fusion.2), kind=kOutput, calls=%fused_computation.2 | convolution fusion | flops 67387392 | bytes 1049088 | tf_op jit(solution)/shard_map/dot_general | solution.py:54
  7.8 0.0 copy-start.1
  7.9 0.2 collective-permute-start
  8.1 2.0 %collective-permute-start.2 = (bf16[64,2048]{1,0:T(8,128)(2,1)S(1)}, bf16[64,2048]{1,0:T(8,128)(2,1)S(1)}, u32[]{:S(2)}, u32[]{:S(2)}) collective-permute-start(bf16[64,2048]{1,0:T(8,128)(2,1)S(1)} %get-tuple-element.3), channel_id=1, source_target_pairs={{0,2},{1,3},{2,0},{3,1},{4,6},{5,7},{6,4},{7,5},{8,10},{9,11},{10,... | collective-permute-start | bytes 786440 | tf_op jit(solution)/shard_map/ppermute | solution.py:15
  10.1 0.0 collective-permute-done.6
  10.1 0.0 collective-permute-done.7
  10.1 0.0 collective-permute-done.8
  10.1 1.6 %collective-permute-start.10 = (f32[2]{0:T(128)S(1)}, f32[2]{0:T(128)S(1)}, u32[]{:S(2)}, u32[]{:S(2)}) collective-permute-start(f32[2]{0:T(128)S(1)} %add_add_fusion), channel_id=1, source_target_pairs={{0,8},{4,12},{8,0},{12,4},{16,24},{20,28},{24,16},{28,20},{1,9},{5... | collective-permute-start | bytes 32 | tf_op jit(solution)/shard_map/ppermute | solution.py:9
  11.8 1.4 %collective-permute-start.11 = (f32[2]{0:T(128)S(1)}, f32[2]{0:T(128)S(1)}, u32[]{:S(2)}, u32[]{:S(2)}) collective-permute-start(f32[2]{0:T(128)S(1)} %add_add_fusion), channel_id=1, source_target_pairs={{0,12},{4,8},{8,4},{12,0},{16,28},{20,24},{24,20},{28,16},{1,13},{... | collective-permute-start | bytes 32 | tf_op jit(solution)/shard_map/ppermute | solution.py:9
  13.2 2.6 %collective-permute-start.12 = (f32[2]{0:T(128)S(1)}, f32[2]{0:T(128)S(1)}, u32[]{:S(2)}, u32[]{:S(2)}) collective-permute-start(f32[2]{0:T(128)S(1)} %add_add_fusion), channel_id=1, source_target_pairs={{0,16},{4,20},{8,24},{12,28},{16,0},{20,4},{24,8},{28,12},{1,17},{... | collective-permute-start | bytes 32 | tf_op jit(solution)/shard_map/ppermute | solution.py:9
  15.8 1.5 %collective-permute-start.13 = (f32[2]{0:T(128)S(1)}, f32[2]{0:T(128)S(1)}, u32[]{:S(2)}, u32[]{:S(2)}) collective-permute-start(f32[2]{0:T(128)S(1)} %add_add_fusion), channel_id=1, source_target_pairs={{0,20},{4,16},{8,28},{12,24},{16,4},{20,0},{24,12},{28,8},{1,21},{... | collective-permute-start | bytes 32 | tf_op jit(solution)/shard_map/ppermute | solution.py:9
  17.3 0.0 collective-permute-done.11
  17.3 2.3 %collective-permute-start.14 = (f32[2]{0:T(128)S(1)}, f32[2]{0:T(128)S(1)}, u32[]{:S(2)}, u32[]{:S(2)}) collective-permute-start(f32[2]{0:T(128)S(1)} %add_add_fusion), channel_id=1, source_target_pairs={{0,24},{4,28},{8,16},{12,20},{16,8},{20,12},{24,0},{28,4},{1,25},{... | collective-permute-start | bytes 32 | tf_op jit(solution)/shard_map/ppermute | solution.py:9
  19.7 1.5 %collective-permute-start.15 = (f32[2]{0:T(128)S(1)}, f32[2]{0:T(128)S(1)}, u32[]{:S(2)}, u32[]{:S(2)}) collective-permute-start(f32[2]{0:T(128)S(1)} %add_add_fusion), channel_id=1, source_target_pairs={{0,28},{4,24},{8,20},{12,16},{16,12},{20,8},{24,4},{28,0},{1,29},{... | collective-permute-start | bytes 32 | tf_op jit(solution)/shard_map/ppermute | solution.py:9
  21.2 0.0 collective-permute-done.13
  21.2 1.5 %collective-permute-start.9 = (f32[2]{0:T(128)S(1)}, f32[2]{0:T(128)S(1)}, u32[]{:S(2)}, u32[]{:S(2)}) collective-permute-start(f32[2]{0:T(128)S(1)} %add_add_fusion), channel_id=1, source_target_pairs={{0,4},{4,0},{8,12},{12,8},{16,20},{20,16},{24,28},{28,24},{1,5},{5... | collective-permute-start | bytes 32 | tf_op jit(solution)/shard_map/ppermute | solution.py:9
  22.7 0.0 collective-permute-done.14
  22.7 3.2 %collective-permute-done.15 = f32[2]{0:T(128)S(1)} collective-permute-done((f32[2]{0:T(128)S(1)}, f32[2]{0:T(128)S(1)}, u32[]{:S(2)}, u32[]{:S(2)}) %collective-permute-start.15) | collective-permute-done | bytes 40 | tf_op jit(solution)/shard_map/ppermute | solution.py:9
  25.9 0.5 add_multiply_fusion
  26.4 0.0 collective-permute-done.2
  26.5 0.0 collective-permute-start.3
  26.5 0.7 %copy-done.4 = bf16[64,2048]{1,0:T(8,128)(2,1)} copy-done((bf16[64,2048]{1,0:T(8,128)(2,1)}, bf16[64,2048]{1,0:T(8,128)(2,1)S(1)}, u32[]{:S(2)}) %copy-start.4) | copy-done | bytes 262168
  27.2 3.2 %fusion.7 = f32[128,768]{1,0:T(8,128)} fusion(bf16[2048,768]{1,0:T(8,128)(2,1)} %param.11, bf16[64,2048]{1,0:T(8,128)(2,1)S(1)} %collective-permute-done, bf16[64,2048]{1,0:T(8,128)(2,1)S(1)} %get-tuple-element.2), kind=kOutput, calls=%fused_computation.16 | convolution fusion | flops 403701760 | bytes 4063232 | tf_op jit(solution)/shard_map/dot_general | solution.py:26
  30.5 0.0 copy-start.2
  30.5 0.8 %copy-done.2 = bf16[128,2048]{1,0:T(8,128)(2,1)} copy-done((bf16[128,2048]{1,0:T(8,128)(2,1)}, bf16[128,2048]{1,0:T(8,128)(2,1)S(1)}, u32[]{:S(2)}) %copy-start.2) | copy-done | bytes 524312
  31.3 0.6 %fusion.29 = f32[128,768]{1,0:T(8,128)S(1)} fusion(bf16[128,2048]{1,0:T(8,128)(2,1)S(1)} %constant_dynamic-update-slice_fusion, bf16[2048,768]{1,0:T(8,128)(2,1)S(1)} %copy-done.1), kind=kOutput, calls=%fused_computation.50 | convolution fusion | flops 402653184 | bytes 4063232 | tf_op jit(solution)/shard_map/dot_general | solution.py:26
  31.9 4.3 %fusion.9 = f32[128,2048]{1,0:T(8,128)} fusion(bf16[768,2048]{1,0:T(8,128)(2,1)S(1)} %copy-done, f32[128,768]{1,0:T(8,128)S(1)} %fusion.29, bf16[128,2048]{1,0:T(8,128)(2,1)} %copy-done.2, bf16[2048,768]{1,0:T(8,128)(2,1)} %param.12), kind=kOutput, calls=%fused_computation.18 | convolution fusion | flops 805896192 | bytes 8257536 | tf_op jit(solution)/shard_map/dot_general | solution.py:29
  36.2 1.1 %slice.42 = bf16[64,2048]{1,0:T(8,128)(2,1)S(1)} slice(f32[128,2048]{1,0:T(8,128)} %fusion.9), slice={[64:128], [0:2048]} | slice | bytes 524288 | tf_op jit(solution)/shard_map/slice | solution.py:68
  37.3 0.0 copy-start.5
  37.3 0.6 %collective-permute-start.4 = (bf16[64,2048]{1,0:T(8,128)(2,1)S(1)}, bf16[64,2048]{1,0:T(8,128)(2,1)}, u32[]{:S(2)}, u32[]{:S(2)}) collective-permute-start(bf16[64,2048]{1,0:T(8,128)(2,1)S(1)} %slice.42), channel_id=1, source_target_pairs={{0,1},{1,0},{2,3},{3,2},{4,5},{5,4},{6,7},{7,6},{8,9},{9,8},{10,11... | collective-permute-start | bytes 786440 | tf_op jit(solution)/shard_map/ppermute | solution.py:9
  37.8 4.4 %fusion.8 = f32[128,2048]{1,0:T(8,128)} fusion(bf16[768,2048]{1,0:T(8,128)(2,1)S(1)} %copy-done, f32[128,768]{1,0:T(8,128)} %fusion.7, bf16[2048,768]{1,0:T(8,128)(2,1)} %param.12, bf16[64,2048]{1,0:T(8,128)(2,1)} %copy-done.4, bf16[64,2048]{1,0:T(8,128)(2,1)} %copy-done.3), kind=kOutput, calls=%fused_computation.17 | convolution fusion | flops 806944768 | bytes 8257536 | tf_op jit(solution)/shard_map/dot_general | solution.py:29
  42.2 1.1 %slice.43 = bf16[64,2048]{1,0:T(8,128)(2,1)S(1)} slice(f32[128,2048]{1,0:T(8,128)} %fusion.8), slice={[64:128], [0:2048]} | slice | bytes 524288 | tf_op jit(solution)/shard_map/slice | solution.py:68
  43.3 0.1 collective-permute-start.1
  43.4 1.2 %fusion.1 = bf16[64,2048]{1,0:T(8,128)(2,1)S(1)} fusion(f32[128,2048]{1,0:T(8,128)} %fusion.9, bf16[64,2048]{1,0:T(8,128)(2,1)} %collective-permute-done.4), kind=kLoop, calls=%fused_computation.5 | loop fusion | flops 393216 | bytes 1048576 | tf_op jit(solution)/shard_map/convert_element_type | solution.py:69
  44.5 0.6 %collective-permute-start.5 = (bf16[64,2048]{1,0:T(8,128)(2,1)S(1)}, bf16[64,2048]{1,0:T(8,128)(2,1)S(1)}, u32[]{:S(2)}, u32[]{:S(2)}) collective-permute-start(bf16[64,2048]{1,0:T(8,128)(2,1)S(1)} %fusion.1), channel_id=1, source_target_pairs={{0,2},{1,3},{2,0},{3,1},{4,6},{5,7},{6,4},{7,5},{8,10},{9,11},{10,... | collective-permute-start | bytes 786440 | tf_op jit(solution)/shard_map/ppermute | solution.py:15
  45.1 1.1 %fusion.2 = bf16[64,2048]{1,0:T(8,128)(2,1)S(1)} fusion(f32[128,2048]{1,0:T(8,128)} %fusion.8, bf16[64,2048]{1,0:T(8,128)(2,1)S(1)} %collective-permute-done.1), kind=kLoop, calls=%fused_computation.8 | loop fusion | flops 393216 | bytes 1048576 | tf_op jit(solution)/shard_map/convert_element_type | solution.py:69
  46.2 7.0 %collective-permute-done.5 = bf16[64,2048]{1,0:T(8,128)(2,1)S(1)} collective-permute-done((bf16[64,2048]{1,0:T(8,128)(2,1)S(1)}, bf16[64,2048]{1,0:T(8,128)(2,1)S(1)}, u32[]{:S(2)}, u32[]{:S(2)}) %collective-permute-start.5) | collective-permute-done | bytes 262176 | tf_op jit(solution)/shard_map/ppermute | solution.py:15
  53.3 1.1 %fusion = bf16[128,2048]{1,0:T(8,128)(2,1)} fusion(bf16[64,2048]{1,0:T(8,128)(2,1)S(1)} %collective-permute-done.5, bf16[64,2048]{1,0:T(8,128)(2,1)S(1)} %fusion.2, f32[128]{0:T(128)S(1)} %bitcast.26, s32[128]{0:T(128)S(1)} %fusion.16), kind=kOutput, calls=%fused_computation.1 | convolution fusion | flops 68698112 | bytes 1049600 | tf_op jit(solution)/shard_map/dot_general | solution.py:78
  (19 shorter events, 0.1 us)
Async XLA Ops:
  0.6 31.2 %copy-start = (bf16[768,2048]{1,0:T(8,128)(2,1)S(1)}, bf16[768,2048]{1,0:T(8,128)(2,1)}, u32[]{:S(2)}) copy-start(bf16[768,2048]{1,0:T(8,128)(2,1)} %param.13) | copy-start | bytes 9437188
  3.4 6.7 %collective-permute-start.6 = (f32[2]{0:T(128)S(1)}, f32[2]{0:T(128)S(1)}, u32[]{:S(2)}, u32[]{:S(2)}) collective-permute-start(f32[2]{0:T(128)S(1)} %fusion.15), channel_id=1, source_target_pairs={{0,1},{1,0},{2,3},{3,2},{4,5},{5,4},{6,7},{7,6},{8,9},{9,8},{10,11... | collective-permute-start | bytes 32 | tf_op jit(solution)/shard_map/ppermute | solution.py:9
  3.9 6.2 %collective-permute-start.7 = (f32[2]{0:T(128)S(1)}, f32[2]{0:T(128)S(1)}, u32[]{:S(2)}, u32[]{:S(2)}) collective-permute-start(f32[2]{0:T(128)S(1)} %fusion.15), channel_id=1, source_target_pairs={{0,2},{1,3},{2,0},{3,1},{4,6},{5,7},{6,4},{7,5},{8,10},{9,11},{10,... | collective-permute-start | bytes 32 | tf_op jit(solution)/shard_map/ppermute | solution.py:9
  6.5 3.6 %collective-permute-start.8 = (f32[2]{0:T(128)S(1)}, f32[2]{0:T(128)S(1)}, u32[]{:S(2)}, u32[]{:S(2)}) collective-permute-start(f32[2]{0:T(128)S(1)} %fusion.15), channel_id=1, source_target_pairs={{0,3},{1,2},{2,1},{3,0},{4,7},{5,6},{6,5},{7,4},{8,11},{9,10},{10,... | collective-permute-start | bytes 32 | tf_op jit(solution)/shard_map/ppermute | solution.py:9
  7.8 23.4 %copy-start.1 = (bf16[2048,768]{1,0:T(8,128)(2,1)S(1)}, bf16[2048,768]{1,0:T(8,128)(2,1)}, u32[]{:S(2)}) copy-start(bf16[2048,768]{1,0:T(8,128)(2,1)} %param.11) | copy-start | bytes 9437188
  7.9 18.6 %copy-start.3 = (bf16[64,2048]{1,0:T(8,128)(2,1)}, bf16[64,2048]{1,0:T(8,128)(2,1)S(1)}, u32[]{:S(2)}) copy-start(bf16[64,2048]{1,0:T(8,128)(2,1)S(1)} %get-tuple-element.2) | copy-start | bytes 786436
  7.9 18.5 %collective-permute-start = (bf16[64,2048]{1,0:T(8,128)(2,1)S(1)}, bf16[64,2048]{1,0:T(8,128)(2,1)S(1)}, u32[]{:S(2)}, u32[]{:S(2)}) collective-permute-start(bf16[64,2048]{1,0:T(8,128)(2,1)S(1)} %get-tuple-element.2), channel_id=1, source_target_pairs={{0,1},{1,0},{2,3},{3,2},{4,5},{5,4},{6,7},{7,6},{8,9},{9,8},{10,11... | collective-permute-start | bytes 786440 | tf_op jit(solution)/shard_map/ppermute | solution.py:9
  8.1 18.3 %collective-permute-start.2 = (bf16[64,2048]{1,0:T(8,128)(2,1)S(1)}, bf16[64,2048]{1,0:T(8,128)(2,1)S(1)}, u32[]{:S(2)}, u32[]{:S(2)}) collective-permute-start(bf16[64,2048]{1,0:T(8,128)(2,1)S(1)} %get-tuple-element.3), channel_id=1, source_target_pairs={{0,2},{1,3},{2,0},{3,1},{4,6},{5,7},{6,4},{7,5},{8,10},{9,11},{10,... | collective-permute-start | bytes 786440 | tf_op jit(solution)/shard_map/ppermute | solution.py:15
  10.1 5.6 %collective-permute-start.10 = (f32[2]{0:T(128)S(1)}, f32[2]{0:T(128)S(1)}, u32[]{:S(2)}, u32[]{:S(2)}) collective-permute-start(f32[2]{0:T(128)S(1)} %add_add_fusion), channel_id=1, source_target_pairs={{0,8},{4,12},{8,0},{12,4},{16,24},{20,28},{24,16},{28,20},{1,9},{5... | collective-permute-start | bytes 32 | tf_op jit(solution)/shard_map/ppermute | solution.py:9
  11.8 5.5 %collective-permute-start.11 = (f32[2]{0:T(128)S(1)}, f32[2]{0:T(128)S(1)}, u32[]{:S(2)}, u32[]{:S(2)}) collective-permute-start(f32[2]{0:T(128)S(1)} %add_add_fusion), channel_id=1, source_target_pairs={{0,12},{4,8},{8,4},{12,0},{16,28},{20,24},{24,20},{28,16},{1,13},{... | collective-permute-start | bytes 32 | tf_op jit(solution)/shard_map/ppermute | solution.py:9
  13.2 6.5 %collective-permute-start.12 = (f32[2]{0:T(128)S(1)}, f32[2]{0:T(128)S(1)}, u32[]{:S(2)}, u32[]{:S(2)}) collective-permute-start(f32[2]{0:T(128)S(1)} %add_add_fusion), channel_id=1, source_target_pairs={{0,16},{4,20},{8,24},{12,28},{16,0},{20,4},{24,8},{28,12},{1,17},{... | collective-permute-start | bytes 32 | tf_op jit(solution)/shard_map/ppermute | solution.py:9
  15.8 5.4 %collective-permute-start.13 = (f32[2]{0:T(128)S(1)}, f32[2]{0:T(128)S(1)}, u32[]{:S(2)}, u32[]{:S(2)}) collective-permute-start(f32[2]{0:T(128)S(1)} %add_add_fusion), channel_id=1, source_target_pairs={{0,20},{4,16},{8,28},{12,24},{16,4},{20,0},{24,12},{28,8},{1,21},{... | collective-permute-start | bytes 32 | tf_op jit(solution)/shard_map/ppermute | solution.py:9
  17.3 5.4 %collective-permute-start.14 = (f32[2]{0:T(128)S(1)}, f32[2]{0:T(128)S(1)}, u32[]{:S(2)}, u32[]{:S(2)}) collective-permute-start(f32[2]{0:T(128)S(1)} %add_add_fusion), channel_id=1, source_target_pairs={{0,24},{4,28},{8,16},{12,20},{16,8},{20,12},{24,0},{28,4},{1,25},{... | collective-permute-start | bytes 32 | tf_op jit(solution)/shard_map/ppermute | solution.py:9
  19.7 6.3 %collective-permute-start.15 = (f32[2]{0:T(128)S(1)}, f32[2]{0:T(128)S(1)}, u32[]{:S(2)}, u32[]{:S(2)}) collective-permute-start(f32[2]{0:T(128)S(1)} %add_add_fusion), channel_id=1, source_target_pairs={{0,28},{4,24},{8,20},{12,16},{16,12},{20,8},{24,4},{28,0},{1,29},{... | collective-permute-start | bytes 32 | tf_op jit(solution)/shard_map/ppermute | solution.py:9
  21.2 4.7 %collective-permute-start.9 = (f32[2]{0:T(128)S(1)}, f32[2]{0:T(128)S(1)}, u32[]{:S(2)}, u32[]{:S(2)}) collective-permute-start(f32[2]{0:T(128)S(1)} %add_add_fusion), channel_id=1, source_target_pairs={{0,4},{4,0},{8,12},{12,8},{16,20},{20,16},{24,28},{28,24},{1,5},{5... | collective-permute-start | bytes 32 | tf_op jit(solution)/shard_map/ppermute | solution.py:9
  26.5 4.0 %collective-permute-start.3 = (bf16[64,2048]{1,0:T(8,128)(2,1)S(1)}, bf16[64,2048]{1,0:T(8,128)(2,1)S(1)}, u32[]{:S(2)}, u32[]{:S(2)}) collective-permute-start(bf16[64,2048]{1,0:T(8,128)(2,1)S(1)} %collective-permute-done.2), channel_id=1, source_target_pairs={{0,1},{1,0},{2,3},{3,2},{4,5},{5,4},{6,7},{7,6},{8,9},{9,8},{10,11... | collective-permute-start | bytes 786440 | tf_op jit(solution)/shard_map/ppermute | solution.py:9
  26.5 0.7 %copy-start.4 = (bf16[64,2048]{1,0:T(8,128)(2,1)}, bf16[64,2048]{1,0:T(8,128)(2,1)S(1)}, u32[]{:S(2)}) copy-start(bf16[64,2048]{1,0:T(8,128)(2,1)S(1)} %collective-permute-done) | copy-start | bytes 786436
  30.5 0.8 %copy-start.2 = (bf16[128,2048]{1,0:T(8,128)(2,1)}, bf16[128,2048]{1,0:T(8,128)(2,1)S(1)}, u32[]{:S(2)}) copy-start(bf16[128,2048]{1,0:T(8,128)(2,1)S(1)} %constant_dynamic-update-slice_fusion) | copy-start | bytes 1572868
  37.3 16.0 %copy-start.5 = (f32[128,1]{0,1:T(1,128)S(1)}, f32[128,1]{0,1:T(1,128)}, u32[]{:S(2)}) copy-start(f32[128,1]{0,1:T(1,128)} %param.10) | copy-start | bytes 1540
  37.3 6.1 %collective-permute-start.4 = (bf16[64,2048]{1,0:T(8,128)(2,1)S(1)}, bf16[64,2048]{1,0:T(8,128)(2,1)}, u32[]{:S(2)}, u32[]{:S(2)}) collective-permute-start(bf16[64,2048]{1,0:T(8,128)(2,1)S(1)} %slice.42), channel_id=1, source_target_pairs={{0,1},{1,0},{2,3},{3,2},{4,5},{5,4},{6,7},{7,6},{8,9},{9,8},{10,11... | collective-permute-start | bytes 786440 | tf_op jit(solution)/shard_map/ppermute | solution.py:9
  43.3 1.9 %collective-permute-start.1 = (bf16[64,2048]{1,0:T(8,128)(2,1)S(1)}, bf16[64,2048]{1,0:T(8,128)(2,1)S(1)}, u32[]{:S(2)}, u32[]{:S(2)}) collective-permute-start(bf16[64,2048]{1,0:T(8,128)(2,1)S(1)} %slice.43), channel_id=1, source_target_pairs={{0,1},{1,0},{2,3},{3,2},{4,5},{5,4},{6,7},{7,6},{8,9},{9,8},{10,11... | collective-permute-start | bytes 786440 | tf_op jit(solution)/shard_map/ppermute | solution.py:9
  44.5 8.8 %collective-permute-start.5 = (bf16[64,2048]{1,0:T(8,128)(2,1)S(1)}, bf16[64,2048]{1,0:T(8,128)(2,1)S(1)}, u32[]{:S(2)}, u32[]{:S(2)}) collective-permute-start(bf16[64,2048]{1,0:T(8,128)(2,1)S(1)} %fusion.1), channel_id=1, source_target_pairs={{0,2},{1,3},{2,0},{3,1},{4,6},{5,7},{6,4},{7,5},{8,10},{9,11},{10,... | collective-permute-start | bytes 786440 | tf_op jit(solution)/shard_map/ppermute | solution.py:15

commit v2 on v1

v2 whole, which is shorter than its diff:
```python
import functools

import jax
import jax.numpy as jnp
from jax import lax
from jax.experimental import pallas as pl
from jax.experimental.pallas import tpu as pltpu
from jax.sharding import PartitionSpec as P

VMEM = pl.BlockSpec(memory_space=pltpu.VMEM)


def swap(value, axis, mask):
    pairs = [(source, source ^ mask) for source in range(lax.axis_size(axis))]
    return lax.ppermute(value, axis, pairs)


def shift(value, step):
    members = lax.axis_size("expert")
    pairs = [(source, (source + 2 * step) % members) for source in range(members)]
    return lax.ppermute(value, "expert", pairs)


def pack_kernel(experts, capacity, ids_ref, copy_ref, gate_ref, tokens_ref, target_ref, load_ref, *packed_refs):
    chosen, tok_rows = ids_ref.shape
    rows = 2 * capacity
    sections = 2 * experts
    own = lax.axis_index("expert") // 2
    section = lax.broadcasted_iota(jnp.int32, (max(16, sections), tok_rows), 0)
    keys, hots = [], []
    for k in range(chosen):
        relative = ids_ref[k : k + 1, :] - own
        relative = jnp.where(relative < 0, relative + experts, relative)
        keys.append(relative * 2 + copy_ref[k : k + 1, :])
        hots.append(jnp.where(section == keys[k], 1.0, 0.0))
    total = functools.reduce(lambda a, b: a + b, hots)
    earlier = lax.broadcasted_iota(jnp.int32, (tok_rows, tok_rows), 0) < lax.broadcasted_iota(
        jnp.int32, (tok_rows, tok_rows), 1
    )
    before = jnp.dot(
        total.astype(jnp.bfloat16),
        jnp.where(earlier, 1.0, 0.0).astype(jnp.bfloat16),
        preferred_element_type=jnp.float32,
    )
    targets = []
    served = lax.broadcasted_iota(jnp.int32, (load_ref.shape[0], tok_rows), 0)
    load = jnp.zeros((load_ref.shape[0], tok_rows), jnp.float32)
    for k in range(chosen):
        rank = jnp.sum(before * hots[k], axis=0, keepdims=True).astype(jnp.int32)
        before = before + hots[k]
        retained = rank < capacity
        target = jnp.where(retained, keys[k] * capacity + rank, -1)
        targets.append(target)
        target_ref[k : k + 1, :] = target
        kept = jnp.where(retained, gate_ref[k : k + 1, :], 0.0)
        load = load + jnp.where(served == ids_ref[k : k + 1, :], kept, 0.0)
    load_ref[...] = jnp.broadcast_to(jnp.sum(load, axis=1, keepdims=True), load_ref.shape)
    tokens = tokens_ref[...]
    place = lax.broadcasted_iota(jnp.int32, (rows, tok_rows), 0)
    for step in list(range(1, experts)) + [0]:
        match = functools.reduce(
            lambda a, b: a | b, [place + step * rows == target for target in targets]
        )
        packed = jnp.dot(
            jnp.where(match, 1.0, 0.0).astype(jnp.bfloat16), tokens, preferred_element_type=jnp.float32
        )
        packed_refs[step][...] = packed.astype(jnp.bfloat16)


def expert_kernel(mine_ref, other_ref, gate_ref, up_ref, down_ref, part_ref, send_ref):
    count = mine_ref.shape[0]
    both = jnp.concatenate([mine_ref[...], other_ref[...]], axis=0)
    gate_act = jnp.dot(both, gate_ref[...], preferred_element_type=jnp.float32)
    up_act = jnp.dot(both, up_ref[...], preferred_element_type=jnp.float32)
    hidden = (gate_act / (1.0 + jnp.exp(-gate_act)) * up_act).astype(jnp.bfloat16)
    out = jnp.dot(hidden, down_ref[...], preferred_element_type=jnp.float32)
    part_ref[...] = out[:count]
    send_ref[...] = out[count:].astype(jnp.bfloat16)


def merge_kernel(part_ref, other_ref, out_ref):
    out_ref[...] = (part_ref[...] + other_ref[...].astype(jnp.float32)).astype(jnp.bfloat16)


def combine_kernel(target_ref, gate_ref, *refs):
    result_refs, out_ref = refs[:-1], refs[-1]
    chosen, tok_rows = target_ref.shape
    results = jnp.concatenate([ref[...] for ref in result_refs], axis=0)
    slots = results.shape[0]
    slot = lax.broadcasted_iota(jnp.int32, (tok_rows, slots), 1)
    combined = None
    for k in range(chosen):
        column = jnp.broadcast_to(target_ref[k : k + 1, :], (slots, tok_rows)).T
        scale = jnp.broadcast_to(gate_ref[k : k + 1, :], (128, tok_rows)).T[:, :1]
        select = jnp.where(column == slot, 1.0, 0.0).astype(jnp.bfloat16)
        term = scale * jnp.dot(select, results, preferred_element_type=jnp.float32)
        combined = term if combined is None else combined + term
    out_ref[...] = combined.astype(jnp.bfloat16)


def call(kernel, outs, count, name, megabytes):
    return pl.pallas_call(
        kernel,
        out_shape=outs,
        in_specs=[VMEM] * count,
        out_specs=jax.tree.map(lambda _: VMEM, outs),
        compiler_params=pltpu.CompilerParams(vmem_limit_bytes=megabytes << 20),
        name=name,
    )


def local(tokens, expert_ids, copy_choice, gate_weights, w_gate, w_up, w_down):
    members = lax.axis_size("expert")
    experts = members // 2
    tok_rows, chosen = expert_ids.shape
    features = tokens.shape[1]
    capacity = max(2, tok_rows * chosen // (2 * experts))
    rows = 2 * capacity
    gates = gate_weights.T
    block = jax.ShapeDtypeStruct((rows, features), jnp.bfloat16)
    target, load, *packed = call(
        functools.partial(pack_kernel, experts, capacity),
        [
            jax.ShapeDtypeStruct((chosen, tok_rows), jnp.int32),
            jax.ShapeDtypeStruct((max(8, experts), 128), jnp.float32),
        ]
        + [block] * experts,
        4,
        "pack",
        8,
    )(expert_ids.T, copy_choice.T, gates, tokens)

    def serve(mine, other):
        count = mine.shape[0]
        part, send = call(
            expert_kernel,
            [
                jax.ShapeDtypeStruct((count, features), jnp.float32),
                jax.ShapeDtypeStruct((count, features), jnp.bfloat16),
            ],
            5,
            "experts",
            20,
        )(mine, other, w_gate, w_up, w_down)
        return call(merge_kernel, jax.ShapeDtypeStruct((count, features), jnp.bfloat16), 2, "merge", 4)(
            part, swap(send, "expert", 1)
        )

    def tree(value, axis):
        mask = 1
        while mask < lax.axis_size(axis):
            value = value + swap(value, axis, mask)
            mask *= 2
        return value

    arrived = [shift(packed[step], step) for step in range(1, experts)]
    arrived = arrived[0] if experts == 2 else jnp.concatenate(arrived, axis=0)
    far = serve(arrived, swap(arrived, "expert", 1))
    near = serve(packed[0], swap(packed[0], "expert", 1))
    load_sum = tree(tree(load, "expert"), "dp")
    expert_load = load_sum[:experts, 0] / (tok_rows * lax.axis_size("dp") * members)
    returned = [shift(far[(step - 1) * rows : step * rows], -step) for step in range(1, experts)]
    combined = call(
        combine_kernel, jax.ShapeDtypeStruct((tok_rows, features), jnp.bfloat16), 2 + experts, "combine", 8
    )(target, gates, near, *returned)
    return (combined, expert_load)


def solution(mesh):
    return jax.shard_map(
        local,
        mesh=mesh,
        in_specs=(
            P(("dp", "expert"), None),
            P(("dp", "expert"), None),
            P(("dp", "expert"), None),
            P(("dp", "expert"), None),
            P(None, "expert"),
            P(None, "expert"),
            P("expert", None),
        ),
        out_specs=(P(("dp", "expert"), None), P()),
        check_vma=False,
    )
```

time: 54.8 us -> 46.9 us (0.86)
  matrix products: 14.9 us -> 0 us
  waiting for transfers between devices: 10.3 us -> 19.2 us
  starting transfers between devices: 19.1 us -> 12.6 us
  local copies, waits for them, and re-layouts: 3.75 us -> 8.87 us
  other arithmetic: 5.49 us -> 0.64 us
  Pallas kernels: 0 us -> 4.63 us
    dot_general x6 -> x0, matrix products: 14.9 us -> none  [the longest x2 8.67 us: expert_pass(): return jnp.dot(hidden, weight_down, preferred_element_type=jnp.float32)]
    ppermute x14 -> x9, waiting for transfers between devices: 3.25 us -> 12.8 us  [swap(): return lax.ppermute(value, axis, pairs)]
    ppermute x14 -> x9, starting transfers between devices: 16.6 us -> 7.75 us  [swap(): return lax.ppermute(value, axis, pairs)]
    unnamed x13 -> x18, local copies, waits for them, and re-layouts: 1.55 us -> 8.87 us
    pallas_call x0 -> x6, Pallas kernels: none -> 4.63 us  [the longest x2 2.94 us: serve(): call(expert_kernel, [jax.ShapeDtypeStruct((count, features), jnp.float32)...]
    convert_element_type x3 -> x0, other arithmetic: 2.34 us -> none  [the longest x2 2.26 us: serve(): return (partial[:count] + other.astype(jnp.float32)).astype(jnp.bfloat16)]
    ppermute x2, starting transfers between devices: 2.56 us -> 4.83 us  [shift(): return lax.ppermute(value, 'expert', pairs)]
    slice x3 -> x0, local copies, waits for them, and re-layouts: 2.18 us -> none  [the longest x2 2.14 us: serve(): other = swap(partial[count:].astype(jnp.bfloat16), 'expert', 1)]
  transfers between devices with their start and end apart: 16 -> 11, of which waited for: 2 -> 7; matrix products, arithmetic and copies ran while one was open for 24% -> 1% of each run, Pallas kernels for 0% -> 7%
where the time goes in v2:
time: 46.9 us; the launch traced here: 46.6 us
  waiting for transfers between devices  19.2 us (41%)
  starting transfers between devices  12.6 us (27%)
  local copies, waits for them, and re-layouts  8.87 us (19%)
  Pallas kernels  4.63 us (10%)
  between operations  0.71 us (2%)
  other arithmetic  0.64 us (1%)
    ppermute x9, waiting for transfers between devices, swap(): return lax.ppermute(value, axis, pairs)  12.8 us
    unnamed x18, local copies, waits for them, and re-layouts  8.87 us
    ppermute x9, starting transfers between devices, swap(): return lax.ppermute(value, axis, pairs)  7.75 us
    ppermute x2, waiting for transfers between devices, shift(): return lax.ppermute(value, 'expert', pairs)  6.31 us
    ppermute x2, starting transfers between devices, shift(): return lax.ppermute(value, 'expert', pairs)  4.83 us
    pallas_call x2, Pallas kernels, serve(): call(expert_kernel, [jax.ShapeDtypeStruct((count, features), jnp.float32)...  2.94 us
    pallas_call x1, Pallas kernels, local(): call(combine_kernel, jax.ShapeDtypeStruct((tok_rows, features), jnp.bfloa...  1.15 us
  transfers between devices with their start and end apart: 11, of which 7 were waited for; matrix products, arithmetic and copies ran while one was open for 1% of the time, Pallas kernels for 7%

profile of v2, /device:TPU:0, one launch (start us, length us, event | category | flops | bytes accessed | tf_op | source)
XLA Modules:
  0.0 46.6 jit_solution(17200496867336815392)
XLA Ops:
  0.6 0.0 copy-start.4
  0.6 1.0 %copy-done.4 = bf16[128,2048]{1,0:T(8,128)(2,1)S(1)} copy-done((bf16[128,2048]{1,0:T(8,128)(2,1)S(1)}, bf16[128,2048]{1,0:T(8,128)(2,1)}, u32[]{:S(2)}) %copy-start.4) | copy-done | bytes 524312
  1.7 0.0 copy-start.5
  1.7 0.7 %copy-done.5 = f32[128,1]{0,1:T(1,128)S(1)} copy-done((f32[128,1]{0,1:T(1,128)S(1)}, f32[128,1]{0,1:T(1,128)}, u32[]{:S(2)}) %copy-start.5) | copy-done | bytes 536
  2.3 0.0 copy-start.7
  2.3 0.7 %copy-done.7 = s32[128,1]{0,1:T(1,128)S(1)} copy-done((s32[128,1]{0,1:T(1,128)S(1)}, s32[128,1]{0,1:T(1,128)}, u32[]{:S(2)}) %copy-start.7) | copy-done | bytes 536
  3.0 0.0 copy-start.8
  3.0 0.7 %copy-done.8 = s32[128,1]{0,1:T(1,128)S(1)} copy-done((s32[128,1]{0,1:T(1,128)S(1)}, s32[128,1]{0,1:T(1,128)}, u32[]{:S(2)}) %copy-start.8) | copy-done | bytes 536
  3.6 0.4 pack.1
  4.1 3.0 %collective-permute-start.2 = (bf16[64,2048]{1,0:T(8,128)(2,1)S(1)}, bf16[64,2048]{1,0:T(8,128)(2,1)S(1)}, u32[]{:S(2)}, u32[]{:S(2)}) collective-permute-start(bf16[64,2048]{1,0:T(8,128)(2,1)S(1)} %get-tuple-element.14), channel_id=1, source_target_pairs={{0,2},{1,3},{2,0},{3,1},{4,6},{5,7},{6,4},{7,5},{8,10},{9,11},{10,... | collective-permute-start | bytes 786440 | tf_op jit(solution)/shard_map/ppermute | solution.py:21
  7.1 6.3 %collective-permute-done.2.mine_ref = bf16[64,2048]{1,0:T(8,128)(2,1)S(1)} collective-permute-done((bf16[64,2048]{1,0:T(8,128)(2,1)S(1)}, bf16[64,2048]{1,0:T(8,128)(2,1)S(1)}, u32[]{:S(2)}, u32[]{:S(2)}) %collective-permute-start.2) | collective-permute-done | bytes 262176 | tf_op jit(solution)/shard_map/ppermute | solution.py:21
  13.4 0.0 collective-permute-start.3
  13.4 0.5 %collective-permute-start = (bf16[64,2048]{1,0:T(8,128)(2,1)S(1)}, bf16[64,2048]{1,0:T(8,128)(2,1)S(1)}, u32[]{:S(2)}, u32[]{:S(2)}) collective-permute-start(bf16[64,2048]{1,0:T(8,128)(2,1)S(1)} %get-tuple-element.11.mine_ref), channel_id=1, source_target_pairs={{0,1},{1,0},{2,3},{3,2},{4,5},{5,4},{6,7},{7,6},{8,9},{9,8},{10,11... | collective-permute-start | bytes 786440 | tf_op jit(solution)/shard_map/ppermute | solution.py:15
  13.9 1.0 %collective-permute-done.3.other_ref = bf16[64,2048]{1,0:T(8,128)(2,1)S(1)} collective-permute-done((bf16[64,2048]{1,0:T(8,128)(2,1)S(1)}, bf16[64,2048]{1,0:T(8,128)(2,1)S(1)}, u32[]{:S(2)}, u32[]{:S(2)}) %collective-permute-start.3) | collective-permute-done | bytes 262176 | tf_op jit(solution)/shard_map/ppermute | solution.py:15
  14.9 0.0 copy-start
  14.9 1.9 %copy-done = bf16[2048,768]{1,0:T(8,128)(2,1)S(1)} copy-done((bf16[2048,768]{1,0:T(8,128)(2,1)S(1)}, bf16[2048,768]{1,0:T(8,128)(2,1)}, u32[]{:S(2)}) %copy-start) | copy-done | bytes 3145752
  16.8 0.0 copy-start.2
  16.8 1.9 %copy-done.2 = bf16[2048,768]{1,0:T(8,128)(2,1)S(1)} copy-done((bf16[2048,768]{1,0:T(8,128)(2,1)S(1)}, bf16[2048,768]{1,0:T(8,128)(2,1)}, u32[]{:S(2)}) %copy-start.2) | copy-done | bytes 3145752
  18.7 0.0 copy-start.3
  18.7 1.9 %copy-done.3 = bf16[768,2048]{1,0:T(8,128)(2,1)S(1)} copy-done((bf16[768,2048]{1,0:T(8,128)(2,1)S(1)}, bf16[768,2048]{1,0:T(8,128)(2,1)}, u32[]{:S(2)}) %copy-start.3) | copy-done | bytes 3145752
  20.6 0.0 copy-start.1
  20.6 1.5 %experts.3 = (f32[64,2048]{1,0:T(8,128)S(1)}, bf16[64,2048]{1,0:T(8,128)(2,1)S(1)}) custom-call(bf16[64,2048]{1,0:T(8,128)(2,1)S(1)} %collective-permute-done.2.mine_ref, bf16[64,2048]{1,0:T(8,128)(2,1)S(1)} %collective-permute-done.3.other_ref, bf16[2048,768]{1,0:T(8,128)(2,1)S(1)} %copy-done, bf16[2048,768]{1,0:T(8,128)(2,1)S(1)} %copy-done.2, ...), custom_call_target="tpu_custom_call" | custom-call | tf_op jit(solution)/shard_map/experts/pallas_call | solution.py:135
  22.1 0.0 copy-start.6
  22.1 0.2 collective-permute-start.4
  22.3 0.0 collective-permute-done.other_ref
  22.3 0.2 copy-done.1
  22.5 1.5 %experts.2 = (f32[64,2048]{1,0:T(8,128)S(1)}, bf16[64,2048]{1,0:T(8,128)(2,1)S(1)}) custom-call(bf16[64,2048]{1,0:T(8,128)(2,1)S(1)} %get-tuple-element.11.mine_ref, bf16[64,2048]{1,0:T(8,128)(2,1)S(1)} %collective-permute-done.other_ref, bf16[2048,768]{1,0:T(8,128)(2,1)S(1)} %copy-done.1, bf16[2048,768]{1,0:T(8,128)(2,1)S(1)} %copy-done.2, ...), custom_call_target="tpu_custom_call" | custom-call | tf_op jit(solution)/shard_map/experts/pallas_call | solution.py:135
  24.0 0.2 collective-permute-start.1
  24.2 0.0 collective-permute-done.4.other_ref
  24.3 1.8 %collective-permute-start.5 = (bf16[64,2048]{1,0:T(8,128)(2,1)S(1)}, bf16[64,2048]{1,0:T(8,128)(2,1)S(1)}, u32[]{:S(2)}, u32[]{:S(2)}) collective-permute-start(bf16[64,2048]{1,0:T(8,128)(2,1)S(1)} %merge.3), channel_id=1, source_target_pairs={{0,2},{1,3},{2,0},{3,1},{4,6},{5,7},{6,4},{7,5},{8,10},{9,11},{10,... | collective-permute-start | bytes 786440 | tf_op jit(solution)/shard_map/ppermute | solution.py:21
  26.1 0.0 collective-permute-start.6
  26.1 1.1 %collective-permute-done.6 = f32[8,128]{1,0:T(8,128)S(1)} collective-permute-done((f32[8,128]{1,0:T(8,128)S(1)}, f32[8,128]{1,0:T(8,128)S(1)}, u32[]{:S(2)}, u32[]{:S(2)}) %collective-permute-start.6) | collective-permute-done | bytes 4128 | tf_op jit(solution)/shard_map/ppermute | solution.py:15
  27.3 0.3 collective-permute-start.7
  27.5 5.4 %collective-permute-done.7 = f32[8,128]{1,0:T(8,128)S(1)} collective-permute-done((f32[8,128]{1,0:T(8,128)S(1)}, f32[8,128]{1,0:T(8,128)S(1)}, u32[]{:S(2)}, u32[]{:S(2)}) %collective-permute-start.7) | collective-permute-done | bytes 4128 | tf_op jit(solution)/shard_map/ppermute | solution.py:15
  33.0 1.8 %collective-permute-start.8 = (f32[8,128]{1,0:T(8,128)S(1)}, f32[8,128]{1,0:T(8,128)S(1)}, u32[]{:S(2)}, u32[]{:S(2)}) collective-permute-start(f32[8,128]{1,0:T(8,128)S(1)} %add.16), channel_id=1, source_target_pairs={{0,4},{4,0},{8,12},{12,8},{16,20},{20,16},{24,28},{28,24},{1,5},{5... | collective-permute-start | bytes 12296 | tf_op jit(solution)/shard_map/ppermute | solution.py:15
  34.8 1.8 %collective-permute-done.8 = f32[8,128]{1,0:T(8,128)S(1)} collective-permute-done((f32[8,128]{1,0:T(8,128)S(1)}, f32[8,128]{1,0:T(8,128)S(1)}, u32[]{:S(2)}, u32[]{:S(2)}) %collective-permute-start.8) | collective-permute-done | bytes 4128 | tf_op jit(solution)/shard_map/ppermute | solution.py:15
  36.6 1.8 %collective-permute-start.9 = (f32[8,128]{1,0:T(8,128)S(1)}, f32[8,128]{1,0:T(8,128)S(1)}, u32[]{:S(2)}, u32[]{:S(2)}) collective-permute-start(f32[8,128]{1,0:T(8,128)S(1)} %add.17), channel_id=1, source_target_pairs={{0,8},{4,12},{8,0},{12,4},{16,24},{20,28},{24,16},{28,20},{1,9},{5... | collective-permute-start | bytes 12296 | tf_op jit(solution)/shard_map/ppermute | solution.py:15
  38.4 1.8 %collective-permute-done.9 = f32[8,128]{1,0:T(8,128)S(1)} collective-permute-done((f32[8,128]{1,0:T(8,128)S(1)}, f32[8,128]{1,0:T(8,128)S(1)}, u32[]{:S(2)}, u32[]{:S(2)}) %collective-permute-start.9) | collective-permute-done | bytes 4128 | tf_op jit(solution)/shard_map/ppermute | solution.py:15
  40.2 2.9 %collective-permute-start.10 = (f32[8,128]{1,0:T(8,128)S(1)}, f32[8,128]{1,0:T(8,128)S(1)}, u32[]{:S(2)}, u32[]{:S(2)}) collective-permute-start(f32[8,128]{1,0:T(8,128)S(1)} %add.18), channel_id=1, source_target_pairs={{0,16},{4,20},{8,24},{12,28},{16,0},{20,4},{24,8},{28,12},{1,17},{... | collective-permute-start | bytes 12296 | tf_op jit(solution)/shard_map/ppermute | solution.py:15
  43.1 1.7 %collective-permute-done.10 = f32[8,128]{1,0:T(8,128)S(1)} collective-permute-done((f32[8,128]{1,0:T(8,128)S(1)}, f32[8,128]{1,0:T(8,128)S(1)}, u32[]{:S(2)}, u32[]{:S(2)}) %collective-permute-start.10) | collective-permute-done | bytes 4128 | tf_op jit(solution)/shard_map/ppermute | solution.py:15
  44.7 0.6 %multiply_reduce_fusion = f32[2]{0:T(128)} fusion(f32[8,128]{1,0:T(8,128)S(1)} %add.19), kind=kLoop, calls=%fused_computation | loop fusion | flops 2 | bytes 16 | tf_op jit(solution)/shard_map/div | solution.py:161
  45.3 0.0 collective-permute-done.1.other_ref
  45.3 0.1 merge.2.refs_0_
  45.4 0.0 collective-permute-done.5.refs_1_
  45.4 0.0 copy-done.6
  45.4 1.1 %combine.1 = bf16[128,2048]{1,0:T(8,128)(2,1)} custom-call(s32[1,128]{1,0:T(1,128)S(1)} %get-tuple-element.10.target_ref, f32[1,128]{1,0:T(1,128)S(1)} %bitcast.4, bf16[64,2048]{1,0:T(8,128)(2,1)S(1)} %merge.2.refs_0_, bf16[64,2048]{1,0:T(8,128)(2,1)S(1)} %collective-permute-done.5.refs_1_), custom_call_target="tpu_custom_call" | custom-call | tf_op jit(solution)/shard_map/combine/pallas_call | solution.py:163
  (6 shorter events, 0.1 us)
Async XLA Ops:
  0.6 1.0 %copy-start.4 = (bf16[128,2048]{1,0:T(8,128)(2,1)S(1)}, bf16[128,2048]{1,0:T(8,128)(2,1)}, u32[]{:S(2)}) copy-start(bf16[128,2048]{1,0:T(8,128)(2,1)} %tokens_ref.1) | copy-start | bytes 1572868
  1.7 0.7 %copy-start.5 = (f32[128,1]{0,1:T(1,128)S(1)}, f32[128,1]{0,1:T(1,128)}, u32[]{:S(2)}) copy-start(f32[128,1]{0,1:T(1,128)} %param.10) | copy-start | bytes 1540
  2.3 0.7 %copy-start.7 = (s32[128,1]{0,1:T(1,128)S(1)}, s32[128,1]{0,1:T(1,128)}, u32[]{:S(2)}) copy-start(s32[128,1]{0,1:T(1,128)} %param.8) | copy-start | bytes 1540
  3.0 0.7 %copy-start.8 = (s32[128,1]{0,1:T(1,128)S(1)}, s32[128,1]{0,1:T(1,128)}, u32[]{:S(2)}) copy-start(s32[128,1]{0,1:T(1,128)} %param.9) | copy-start | bytes 1540
  4.1 9.3 %collective-permute-start.2 = (bf16[64,2048]{1,0:T(8,128)(2,1)S(1)}, bf16[64,2048]{1,0:T(8,128)(2,1)S(1)}, u32[]{:S(2)}, u32[]{:S(2)}) collective-permute-start(bf16[64,2048]{1,0:T(8,128)(2,1)S(1)} %get-tuple-element.14), channel_id=1, source_target_pairs={{0,2},{1,3},{2,0},{3,1},{4,6},{5,7},{6,4},{7,5},{8,10},{9,11},{10,... | collective-permute-start | bytes 786440 | tf_op jit(solution)/shard_map/ppermute | solution.py:21
  13.4 1.5 %collective-permute-start.3 = (bf16[64,2048]{1,0:T(8,128)(2,1)S(1)}, bf16[64,2048]{1,0:T(8,128)(2,1)S(1)}, u32[]{:S(2)}, u32[]{:S(2)}) collective-permute-start(bf16[64,2048]{1,0:T(8,128)(2,1)S(1)} %collective-permute-done.2.mine_ref), channel_id=1, source_target_pairs={{0,1},{1,0},{2,3},{3,2},{4,5},{5,4},{6,7},{7,6},{8,9},{9,8},{10,11... | collective-permute-start | bytes 786440 | tf_op jit(solution)/shard_map/ppermute | solution.py:15
  13.4 8.9 %collective-permute-start = (bf16[64,2048]{1,0:T(8,128)(2,1)S(1)}, bf16[64,2048]{1,0:T(8,128)(2,1)S(1)}, u32[]{:S(2)}, u32[]{:S(2)}) collective-permute-start(bf16[64,2048]{1,0:T(8,128)(2,1)S(1)} %get-tuple-element.11.mine_ref), channel_id=1, source_target_pairs={{0,1},{1,0},{2,3},{3,2},{4,5},{5,4},{6,7},{7,6},{8,9},{9,8},{10,11... | collective-permute-start | bytes 786440 | tf_op jit(solution)/shard_map/ppermute | solution.py:15
  14.9 1.9 %copy-start = (bf16[2048,768]{1,0:T(8,128)(2,1)S(1)}, bf16[2048,768]{1,0:T(8,128)(2,1)}, u32[]{:S(2)}) copy-start(bf16[2048,768]{1,0:T(8,128)(2,1)} %gate_ref.3) | copy-start | bytes 9437188
  16.8 1.9 %copy-start.2 = (bf16[2048,768]{1,0:T(8,128)(2,1)S(1)}, bf16[2048,768]{1,0:T(8,128)(2,1)}, u32[]{:S(2)}) copy-start(bf16[2048,768]{1,0:T(8,128)(2,1)} %up_ref.3) | copy-start | bytes 9437188
  18.7 1.9 %copy-start.3 = (bf16[768,2048]{1,0:T(8,128)(2,1)S(1)}, bf16[768,2048]{1,0:T(8,128)(2,1)}, u32[]{:S(2)}) copy-start(bf16[768,2048]{1,0:T(8,128)(2,1)} %down_ref.3) | copy-start | bytes 9437188
  20.6 1.9 %copy-start.1 = (bf16[2048,768]{1,0:T(8,128)(2,1)S(1)}, bf16[2048,768]{1,0:T(8,128)(2,1)}, u32[]{:S(2)}) copy-start(bf16[2048,768]{1,0:T(8,128)(2,1)} %gate_ref.3) | copy-start | bytes 9437188
  22.1 23.3 %copy-start.6 = (f32[128,1]{0,1:T(1,128)S(1)}, f32[128,1]{0,1:T(1,128)}, u32[]{:S(2)}) copy-start(f32[128,1]{0,1:T(1,128)} %param.10) | copy-start | bytes 1540
  22.1 2.1 %collective-permute-start.4 = (bf16[64,2048]{1,0:T(8,128)(2,1)S(1)}, bf16[64,2048]{1,0:T(8,128)(2,1)S(1)}, u32[]{:S(2)}, u32[]{:S(2)}) collective-permute-start(bf16[64,2048]{1,0:T(8,128)(2,1)S(1)} %get-tuple-element.16), channel_id=1, source_target_pairs={{0,1},{1,0},{2,3},{3,2},{4,5},{5,4},{6,7},{7,6},{8,9},{9,8},{10,11... | collective-permute-start | bytes 786440 | tf_op jit(solution)/shard_map/ppermute | solution.py:15
  24.0 21.4 %collective-permute-start.1 = (bf16[64,2048]{1,0:T(8,128)(2,1)S(1)}, bf16[64,2048]{1,0:T(8,128)(2,1)S(1)}, u32[]{:S(2)}, u32[]{:S(2)}) collective-permute-start(bf16[64,2048]{1,0:T(8,128)(2,1)S(1)} %get-tuple-element.13), channel_id=1, source_target_pairs={{0,1},{1,0},{2,3},{3,2},{4,5},{5,4},{6,7},{7,6},{8,9},{9,8},{10,11... | collective-permute-start | bytes 786440 | tf_op jit(solution)/shard_map/ppermute | solution.py:15
  24.3 21.1 %collective-permute-start.5 = (bf16[64,2048]{1,0:T(8,128)(2,1)S(1)}, bf16[64,2048]{1,0:T(8,128)(2,1)S(1)}, u32[]{:S(2)}, u32[]{:S(2)}) collective-permute-start(bf16[64,2048]{1,0:T(8,128)(2,1)S(1)} %merge.3), channel_id=1, source_target_pairs={{0,2},{1,3},{2,0},{3,1},{4,6},{5,7},{6,4},{7,5},{8,10},{9,11},{10,... | collective-permute-start | bytes 786440 | tf_op jit(solution)/shard_map/ppermute | solution.py:21
  26.1 1.2 %collective-permute-start.6 = (f32[8,128]{1,0:T(8,128)S(1)}, f32[8,128]{1,0:T(8,128)S(1)}, u32[]{:S(2)}, u32[]{:S(2)}) collective-permute-start(f32[8,128]{1,0:T(8,128)S(1)} %get-tuple-element.17), channel_id=1, source_target_pairs={{0,1},{1,0},{2,3},{3,2},{4,5},{5,4},{6,7},{7,6},{8,9},{9,8},{10,11... | collective-permute-start | bytes 12296 | tf_op jit(solution)/shard_map/ppermute | solution.py:15
  27.3 5.7 %collective-permute-start.7 = (f32[8,128]{1,0:T(8,128)S(1)}, f32[8,128]{1,0:T(8,128)S(1)}, u32[]{:S(2)}, u32[]{:S(2)}) collective-permute-start(f32[8,128]{1,0:T(8,128)S(1)} %add.15), channel_id=1, source_target_pairs={{0,2},{1,3},{2,0},{3,1},{4,6},{5,7},{6,4},{7,5},{8,10},{9,11},{10,... | collective-permute-start | bytes 12296 | tf_op jit(solution)/shard_map/ppermute | solution.py:15
  33.0 3.6 %collective-permute-start.8 = (f32[8,128]{1,0:T(8,128)S(1)}, f32[8,128]{1,0:T(8,128)S(1)}, u32[]{:S(2)}, u32[]{:S(2)}) collective-permute-start(f32[8,128]{1,0:T(8,128)S(1)} %add.16), channel_id=1, source_target_pairs={{0,4},{4,0},{8,12},{12,8},{16,20},{20,16},{24,28},{28,24},{1,5},{5... | collective-permute-start | bytes 12296 | tf_op jit(solution)/shard_map/ppermute | solution.py:15
  36.6 3.6 %collective-permute-start.9 = (f32[8,128]{1,0:T(8,128)S(1)}, f32[8,128]{1,0:T(8,128)S(1)}, u32[]{:S(2)}, u32[]{:S(2)}) collective-permute-start(f32[8,128]{1,0:T(8,128)S(1)} %add.17), channel_id=1, source_target_pairs={{0,8},{4,12},{8,0},{12,4},{16,24},{20,28},{24,16},{28,20},{1,9},{5... | collective-permute-start | bytes 12296 | tf_op jit(solution)/shard_map/ppermute | solution.py:15
  40.2 4.5 %collective-permute-start.10 = (f32[8,128]{1,0:T(8,128)S(1)}, f32[8,128]{1,0:T(8,128)S(1)}, u32[]{:S(2)}, u32[]{:S(2)}) collective-permute-start(f32[8,128]{1,0:T(8,128)S(1)} %add.18), channel_id=1, source_target_pairs={{0,16},{4,20},{8,24},{12,28},{16,0},{20,4},{24,8},{28,12},{1,17},{... | collective-permute-start | bytes 12296 | tf_op jit(solution)/shard_map/ppermute | solution.py:15
